TPU v7x, 512 devices: a whole 4x8x8 slice. The times are simulated.
512 devices in a mesh: row: 32 (over y, z_lo), col: 16 (over z_hi, x, core).
Axes of the slice: x: 4, y: 8, z: 8 (z_hi: 2, z_lo: 4; z = z_hi * 4 + z_lo), core: 2. Of those that a mesh axis runs over, the one named last changes fastest.
Arguments:
- embeddings: bfloat16 [8192, 256], P(('row', 'col')), may hold values from -6 to 6
- labels: bfloat16 [8192, 1024], P(('row', 'col')), may hold values from -6 to 6
- tile_mask: int32 [32, 32], replicated, may hold values 0 or 1
Outputs:
- spread_labels: bfloat16 [8192, 1024], P(('row', 'col'))
Inputs may be any that keep to these rules, and one draw needn't show every extreme that they name: Only the entries tile_mask[i, j] with i < j are read; the tile of blocks i and j (and of j and i) is kept where it is 1.
All inputs are finite; a program needn't handle non-finite values.
Results may differ from a plain program's by a relative error of at most 0.015.
Values may be sent and summed in bfloat16 or wider, within the bound.
A program may use at most 64 MiB of HBM per device.

v0:
```python
import math
import jax
import jax.numpy as jnp
from jax import lax
from jax.sharding import PartitionSpec as P

BLOCK = 256
ITERS = 2
MIXING = 0.9
SHARPNESS = 3.0
EPSILON = 1e-06


def unit_rows(embeddings):
    values = embeddings.astype(jnp.float32)
    return (values * lax.rsqrt(jnp.sum(values * values, axis=1, keepdims=True) + EPSILON)).astype(
        jnp.bfloat16
    )


def symmetric_keep(tile_mask):
    blocks = tile_mask.shape[0]
    block_row = lax.broadcasted_iota(jnp.int32, (blocks, blocks), 0)
    block_col = lax.broadcasted_iota(jnp.int32, (blocks, blocks), 1)
    mirrored = jnp.where(block_row < block_col, tile_mask, tile_mask.T)
    return (jnp.where(block_row == block_col, 1, mirrored), block_row, block_col)


def rotate_rows(values, start):
    total = values.shape[0]
    doubled = jnp.concatenate([values, values], axis=0)
    return lax.dynamic_slice_in_dim(doubled, start, total, 0)


def both_terms(operands):
    row_kernel, col_kernel, part_labels, row_labels = operands
    row_term = jnp.dot(row_kernel, part_labels, preferred_element_type=jnp.float32)
    col_term = lax.dot_general(
        col_kernel, row_labels, (((0,), (0,)), ((), ())), preferred_element_type=jnp.float32
    )
    return (row_term, col_term)


def no_terms(operands):
    row_kernel, col_kernel, part_labels, row_labels = operands
    return (
        jnp.zeros((row_kernel.shape[0], part_labels.shape[1]), jnp.float32),
        jnp.zeros((col_kernel.shape[1], row_labels.shape[1]), jnp.float32),
    )


def shards(embeddings, labels, tile_mask):
    row_count = lax.axis_size("row")
    col_count = lax.axis_size("col")
    row_index = lax.axis_index("row")
    col_index = lax.axis_index("col")
    piece_rows = embeddings.shape[0]
    emb_width = embeddings.shape[1]
    channels = labels.shape[1]
    blocks = tile_mask.shape[0]
    sharpness = SHARPNESS * math.sqrt(emb_width)
    unit_vecs = unit_rows(embeddings)
    row_units = lax.all_gather(unit_vecs, "col", axis=0, tiled=True)
    col_gathered = lax.all_gather(unit_vecs, "row", axis=0, tiled=True)
    row_total = row_units.shape[0]
    col_total = col_gathered.shape[0]
    shift = row_index * piece_rows
    back_shift = col_total - shift
    col_units = rotate_rows(col_gathered, shift)
    unit_count = math.gcd(8, row_count)
    unit_width = col_total // unit_count
    kept_sym, block_row, block_col = symmetric_keep(tile_mask)
    chosen = block_row <= block_col
    tile_table = jnp.where(chosen, kept_sym, 0)
    global_rows = row_index * row_total + jnp.arange(row_total, dtype=jnp.int32)
    row_blocks = global_rows // BLOCK
    block_ids = jnp.arange(blocks, dtype=jnp.int32)
    row_onehot = (row_blocks[:, None] == block_ids[None, :]).astype(jnp.bfloat16)
    row_table = jnp.dot(
        row_onehot, tile_table.astype(jnp.bfloat16), preferred_element_type=jnp.float32
    ).astype(jnp.bfloat16)
    local_cols = (jnp.arange(col_total, dtype=jnp.int32) + shift) % col_total
    global_cols = (
        local_cols // piece_rows * col_count + col_index
    ) * piece_rows + local_cols % piece_rows
    col_blocks = global_cols // BLOCK
    kernels_row = []
    kernels_col = []
    active_flags = []
    col_degree = []
    row_degree = jnp.zeros((row_total,), jnp.float32)
    for column_unit in range(unit_count):
        offset_cols = column_unit * unit_width
        part_units = col_units[offset_cols : offset_cols + unit_width]
        part_blocks = col_blocks[offset_cols : offset_cols + unit_width]
        part_cols = global_cols[offset_cols : offset_cols + unit_width]
        col_onehot = (part_blocks[:, None] == block_ids[None, :]).astype(jnp.bfloat16)
        kept_mask = lax.dot_general(
            row_table, col_onehot, (((1,), (1,)), ((), ())), preferred_element_type=jnp.float32
        )
        cosine = lax.dot_general(
            row_units, part_units, (((1,), (1,)), ((), ())), preferred_element_type=jnp.float32
        )
        distinct = global_rows[:, None] != part_cols[None, :]
        weights = jnp.where(
            distinct, jnp.exp(sharpness * cosine) * kept_mask, jnp.zeros_like(cosine)
        ).astype(jnp.bfloat16)
        active_flags.append(jnp.sum(kept_mask) > 0.0)
        kernels_row.append(weights)
        row_degree = row_degree + jnp.sum(weights, axis=1, dtype=jnp.float32)
        crossing = jnp.where(
            row_blocks[:, None] != part_blocks[None, :], weights, jnp.zeros_like(weights)
        )
        kernels_col.append(crossing)
        col_degree.append(jnp.sum(crossing, axis=0, dtype=jnp.float32))
    degree = lax.psum_scatter(row_degree, "col", scatter_dimension=0, tiled=True)
    col_sums = rotate_rows(jnp.concatenate(col_degree), back_shift)
    degree = degree + lax.psum_scatter(col_sums, "row", scatter_dimension=0, tiled=True)
    inv_root = lax.rsqrt(degree)
    seed_scores = labels.astype(jnp.float32)
    current = seed_scores
    for iteration in range(ITERS):
        scaled = (inv_root[:, None] * current).astype(jnp.bfloat16)
        col_labels = rotate_rows(lax.all_gather(scaled, "row", axis=0, tiled=True), shift)
        row_sum = jnp.zeros((row_total, channels), jnp.float32)
        col_parts = []
        row_labels = lax.all_gather(scaled, "col", axis=0, tiled=True)
        for column_unit in range(unit_count):
            offset_cols = column_unit * unit_width
            part_labels = col_labels[offset_cols : offset_cols + unit_width]
            row_term, col_term = lax.cond(
                active_flags[column_unit],
                both_terms,
                no_terms,
                (kernels_row[column_unit], kernels_col[column_unit], part_labels, row_labels),
            )
            row_sum = row_sum + row_term
            col_parts.append(col_term)
        sent_rows = row_sum.astype(jnp.bfloat16).reshape(col_count, piece_rows, channels)
        arrived = lax.all_to_all(sent_rows, "col", split_axis=0, concat_axis=0, tiled=True)
        spread = jnp.sum(arrived, axis=0, dtype=jnp.float32)
        ordered = rotate_rows(jnp.concatenate(col_parts).astype(jnp.bfloat16), back_shift)
        sent_cols = ordered.reshape(row_count, piece_rows, channels)
        returned = lax.all_to_all(sent_cols, "row", split_axis=0, concat_axis=0, tiled=True)
        spread = spread + jnp.sum(returned, axis=0, dtype=jnp.float32)
        current = MIXING * inv_root[:, None] * spread + (1.0 - MIXING) * seed_scores
    return current.astype(jnp.bfloat16)


def solution(mesh):
    placed = (P(("row", "col"), None), P(("row", "col"), None), P())
    return jax.shard_map(
        shards, mesh=mesh, in_specs=placed, out_specs=P(("row", "col"), None), check_vma=False
    )
```

profile of v0, /device:TPU:16, one launch (start us, length us, event | category | flops | bytes accessed | tf_op | source)
XLA Modules:
  0.0 721.4 jit_solution(1597081947624436445)
XLA Ops:
  8.1 35.3 %all_gather.18 = bf16[256,256]{1,0:T(8,128)(2,1)S(1)} all-gather(bf16[16,256]{1,0:T(8,128)(2,1)S(1)} %fusion.91), channel_id=1, replica_groups=mesh['row'=32,'col'=16] {'col'}, dimensions={0}, use_global_device_ids=true | all-gather | bytes 139264 | tf_op jit(solution)/shard_map/all_gather | solution.py:63
  43.4 67.6 %all_gather.19 = bf16[512,256]{1,0:T(8,128)(2,1)S(1)} all-gather(bf16[16,256]{1,0:T(8,128)(2,1)S(1)} %fusion.91), channel_id=1, replica_groups=mesh['row'=32,'col'=16] {'row'}, dimensions={0}, use_global_device_ids=true | all-gather | bytes 270336 | tf_op jit(solution)/shard_map/all_gather | solution.py:64
  126.9 73.2 %all-reduce.1 = f32[512]{0:T(512)S(1)} all-reduce(f32[512]{0:T(512)S(1)} %dynamic_slice.19), channel_id=3, replica_groups=mesh['row'=32,'col'=16] {'row'}, use_global_device_ids=true, to_apply=%region_18.19.clone | all-reduce | flops 512 | bytes 4096
  200.1 42.8 %all-reduce = f32[256]{0:T(256)S(1)} all-reduce(f32[256]{0:T(256)S(1)} %add_add_fusion), channel_id=2, replica_groups=mesh['row'=32,'col'=16] {'col'}, use_global_device_ids=true, to_apply=%region_9.10.clone | all-reduce | flops 256 | bytes 2048
  248.6 26.9 %all_gather.21 = bf16[256,1024]{1,0:T(8,128)(2,1)S(1)} all-gather(bf16[16,1024]{1,0:T(8,128)(2,1)} %fusion.72), channel_id=1, replica_groups=mesh['row'=32,'col'=16] {'col'}, dimensions={0}, use_global_device_ids=true | all-gather | bytes 557056 | tf_op jit(solution)/shard_map/all_gather | solution.py:127
  275.5 120.4 %all-gather.3.cloned.1.call-done = bf16[512,1024]{1,0:T(8,128)(2,1)} async-done(((bf16[16,1024]{1,0:T(8,128)(2,1)}), bf16[512,1024]{1,0:T(8,128)(2,1)}) %all-gather.3.cloned.1.call-update) | async-done | bytes 1048592 | tf_op jit(solution)/shard_map/all_gather | solution.py:124
  395.9 2.0 fusion.65
  398.0 1.3 conditional.16
  408.1 1.8 conditional.23
  409.8 4.7 add_convert_fusion.1
  414.5 7.0 all-to-all-start
  424.6 11.7 %all-to-all-done = bf16[16,16,1024]{2,1,0:T(8,128)(2,1)S(1)} async-done(((bf16[16,16,1024]{2,1,0:T(8,128)(2,1)}), bf16[16,16,1024]{2,1,0:T(8,128)(2,1)S(1)}, u32[]{:S(2)}, u32[]{:S(2)}) %all-to-all-start) | async-done | bytes 524320 | tf_op jit(solution)/shard_map/all_to_all | solution.py:140
  436.3 17.4 %all-to-all-start.1 = ((bf16[32,16,1024]{2,1,0:T(8,128)(2,1)}), bf16[32,16,1024]{2,1,0:T(8,128)(2,1)S(1)}, u32[]{:S(2)}, u32[]{:S(2)}) async-start(bf16[32,16,1024]{2,1,0:T(8,128)(2,1)} %bitcast.2), calls=%async_computation.1 | async-start | bytes 2097152 | tf_op jit(solution)/shard_map/all_to_all | solution.py:144
  453.9 28.7 %all-to-all-done.1 = bf16[32,16,1024]{2,1,0:T(8,128)(2,1)S(1)} async-done(((bf16[32,16,1024]{2,1,0:T(8,128)(2,1)}), bf16[32,16,1024]{2,1,0:T(8,128)(2,1)S(1)}, u32[]{:S(2)}, u32[]{:S(2)}) %all-to-all-start.1) | async-done | bytes 1048608 | tf_op jit(solution)/shard_map/all_to_all | solution.py:144
  483.5 32.2 %all_gather.23 = bf16[256,1024]{1,0:T(8,128)(2,1)S(1)} all-gather(bf16[16,1024]{1,0:T(8,128)(2,1)} %fusion.70), channel_id=1, replica_groups=mesh['row'=32,'col'=16] {'col'}, dimensions={0}, use_global_device_ids=true | all-gather | bytes 557056 | tf_op jit(solution)/shard_map/all_gather | solution.py:127
  515.7 110.3 %all-gather.5.cloned.1.call-done = bf16[512,1024]{1,0:T(8,128)(2,1)} async-done(((bf16[16,1024]{1,0:T(8,128)(2,1)}), bf16[512,1024]{1,0:T(8,128)(2,1)}) %all-gather.5.cloned.1.call-update) | async-done | bytes 1048592 | tf_op jit(solution)/shard_map/all_gather | solution.py:124
  626.0 2.0 fusion.64
  628.0 1.3 conditional.24
  638.9 1.8 conditional.31
  640.7 4.7 add_convert_fusion
  645.3 7.3 %all-to-all-start.2 = ((bf16[16,16,1024]{2,1,0:T(8,128)(2,1)}), bf16[16,16,1024]{2,1,0:T(8,128)(2,1)S(1)}, u32[]{:S(2)}, u32[]{:S(2)}) async-start(bf16[16,16,1024]{2,1,0:T(8,128)(2,1)} %bitcast.3), calls=%async_computation.2 | async-start | bytes 1048576 | tf_op jit(solution)/shard_map/all_to_all | solution.py:140
  655.8 11.7 %all-to-all-done.2 = bf16[16,16,1024]{2,1,0:T(8,128)(2,1)S(1)} async-done(((bf16[16,16,1024]{2,1,0:T(8,128)(2,1)}), bf16[16,16,1024]{2,1,0:T(8,128)(2,1)S(1)}, u32[]{:S(2)}, u32[]{:S(2)}) %all-to-all-start.2) | async-done | bytes 524320 | tf_op jit(solution)/shard_map/all_to_all | solution.py:140
  667.5 17.4 %all-to-all-start.3 = ((bf16[32,16,1024]{2,1,0:T(8,128)(2,1)}), bf16[32,16,1024]{2,1,0:T(8,128)(2,1)S(1)}, u32[]{:S(2)}, u32[]{:S(2)}) async-start(bf16[32,16,1024]{2,1,0:T(8,128)(2,1)} %bitcast.4), calls=%async_computation.3 | async-start | bytes 2097152 | tf_op jit(solution)/shard_map/all_to_all | solution.py:144
  684.9 28.8 %all-to-all-done.3 = bf16[32,16,1024]{2,1,0:T(8,128)(2,1)S(1)} async-done(((bf16[32,16,1024]{2,1,0:T(8,128)(2,1)}), bf16[32,16,1024]{2,1,0:T(8,128)(2,1)S(1)}, u32[]{:S(2)}, u32[]{:S(2)}) %all-to-all-start.3) | async-done | bytes 1048608 | tf_op jit(solution)/shard_map/all_to_all | solution.py:144
  (197 shorter events, 54.5 us)
Async XLA Ops:
  6.5 389.4 %all-gather.3.cloned.1.call-start = ((), (), s32[]{:S(2)}) async-start(), calls=%async_computation.4 | async-start | bytes 1081344 | tf_op jit(solution)/shard_map/all_gather | solution.py:124
  118.4 124.5 %copy-start.25 = (bf16[16,1024]{1,0:T(8,128)(2,1)S(1)}, bf16[16,1024]{1,0:T(8,128)(2,1)}, u32[]{:S(2)}) copy-start(bf16[16,1024]{1,0:T(8,128)(2,1)} %param.36) | copy-start | bytes 98308
  124.2 2.5 copy-start.12
  124.4 280.0 %copy-start.13 = (bf16[256,64]{0,1:T(8,128)(2,1)}, bf16[256,64]{0,1:T(8,128)(2,1)S(1)}, u32[]{:S(2)}) copy-start(bf16[256,64]{0,1:T(8,128)(2,1)S(1)} %fusion.58) | copy-start | bytes 98308
  124.6 278.3 %copy-start.15 = (bf16[256,64]{0,1:T(8,128)(2,1)}, bf16[256,64]{0,1:T(8,128)(2,1)S(1)}, u32[]{:S(2)}) copy-start(bf16[256,64]{0,1:T(8,128)(2,1)S(1)} %fusion.59) | copy-start | bytes 98308
  124.9 276.5 %copy-start.17 = (bf16[256,64]{0,1:T(8,128)(2,1)}, bf16[256,64]{0,1:T(8,128)(2,1)S(1)}, u32[]{:S(2)}) copy-start(bf16[256,64]{0,1:T(8,128)(2,1)S(1)} %fusion.60) | copy-start | bytes 98308
  125.1 274.8 %copy-start.19 = (bf16[256,64]{0,1:T(8,128)(2,1)}, bf16[256,64]{0,1:T(8,128)(2,1)S(1)}, u32[]{:S(2)}) copy-start(bf16[256,64]{0,1:T(8,128)(2,1)S(1)} %fusion.61) | copy-start | bytes 98308
  125.3 274.0 %copy-start.21 = (bf16[256,64]{0,1:T(8,128)(2,1)}, bf16[256,64]{0,1:T(8,128)(2,1)S(1)}, u32[]{:S(2)}) copy-start(bf16[256,64]{0,1:T(8,128)(2,1)S(1)} %fusion.62) | copy-start | bytes 98308
  125.5 272.4 %copy-start.23 = (bf16[256,64]{0,1:T(8,128)(2,1)}, bf16[256,64]{0,1:T(8,128)(2,1)S(1)}, u32[]{:S(2)}) copy-start(bf16[256,64]{0,1:T(8,128)(2,1)S(1)} %fusion.63) | copy-start | bytes 98308
  126.7 272.6 %copy-start.36 = (bf16[256,64]{0,1:T(8,128)(2,1)}, bf16[256,64]{0,1:T(8,128)(2,1)S(1)}, u32[]{:S(2)}) copy-start(bf16[256,64]{0,1:T(8,128)(2,1)S(1)} %get-tuple-element.465) | copy-start | bytes 98308
  126.7 273.2 %copy-start.34 = (bf16[256,64]{0,1:T(8,128)(2,1)}, bf16[256,64]{0,1:T(8,128)(2,1)S(1)}, u32[]{:S(2)}) copy-start(bf16[256,64]{0,1:T(8,128)(2,1)S(1)} %get-tuple-element.468) | copy-start | bytes 98308
  126.7 274.7 %copy-start.32 = (bf16[256,64]{0,1:T(8,128)(2,1)}, bf16[256,64]{0,1:T(8,128)(2,1)S(1)}, u32[]{:S(2)}) copy-start(bf16[256,64]{0,1:T(8,128)(2,1)S(1)} %get-tuple-element.471) | copy-start | bytes 98308
  126.7 276.2 %copy-start.30 = (bf16[256,64]{0,1:T(8,128)(2,1)}, bf16[256,64]{0,1:T(8,128)(2,1)S(1)}, u32[]{:S(2)}) copy-start(bf16[256,64]{0,1:T(8,128)(2,1)S(1)} %get-tuple-element.474) | copy-start | bytes 98308
  126.7 277.7 %copy-start.28 = (bf16[256,64]{0,1:T(8,128)(2,1)}, bf16[256,64]{0,1:T(8,128)(2,1)S(1)}, u32[]{:S(2)}) copy-start(bf16[256,64]{0,1:T(8,128)(2,1)S(1)} %get-tuple-element.477) | copy-start | bytes 98308
  414.5 21.8 %all-to-all-start = ((bf16[16,16,1024]{2,1,0:T(8,128)(2,1)}), bf16[16,16,1024]{2,1,0:T(8,128)(2,1)S(1)}, u32[]{:S(2)}, u32[]{:S(2)}) async-start(bf16[16,16,1024]{2,1,0:T(8,128)(2,1)} %bitcast.1), calls=%async_computation | async-start | bytes 1048576 | tf_op jit(solution)/shard_map/all_to_all | solution.py:140
  424.6 58.1 %copy-start.26 = (bf16[16,1024]{1,0:T(8,128)(2,1)S(1)}, bf16[16,1024]{1,0:T(8,128)(2,1)}, u32[]{:S(2)}) copy-start(bf16[16,1024]{1,0:T(8,128)(2,1)} %param.36) | copy-start | bytes 98308
  436.3 46.3 %all-to-all-start.1 = ((bf16[32,16,1024]{2,1,0:T(8,128)(2,1)}), bf16[32,16,1024]{2,1,0:T(8,128)(2,1)S(1)}, u32[]{:S(2)}, u32[]{:S(2)}) async-start(bf16[32,16,1024]{2,1,0:T(8,128)(2,1)} %bitcast.2), calls=%async_computation.1 | async-start | bytes 2097152 | tf_op jit(solution)/shard_map/all_to_all | solution.py:144
  453.7 172.3 %all-gather.5.cloned.1.call-start = ((), (), s32[]{:S(2)}) async-start(), calls=%async_computation.5 | async-start | bytes 1081344 | tf_op jit(solution)/shard_map/all_gather | solution.py:124
  453.9 174.1 %copy-start.24 = (bf16[256,64]{0,1:T(8,128)(2,1)S(1)}, bf16[256,64]{0,1:T(8,128)(2,1)}, u32[]{:S(2)}) copy-start(bf16[256,64]{0,1:T(8,128)(2,1)} %copy-done.23) | copy-start | bytes 98308
  515.7 112.3 %copy-start.22 = (bf16[256,64]{0,1:T(8,128)(2,1)S(1)}, bf16[256,64]{0,1:T(8,128)(2,1)}, u32[]{:S(2)}) copy-start(bf16[256,64]{0,1:T(8,128)(2,1)} %copy-done.21) | copy-start | bytes 98308
  515.7 112.3 %copy-start.37 = (bf16[256,64]{0,1:T(8,128)(2,1)S(1)}, bf16[256,64]{0,1:T(8,128)(2,1)}, u32[]{:S(2)}) copy-start(bf16[256,64]{0,1:T(8,128)(2,1)} %copy-done.36) | copy-start | bytes 98308
  645.3 22.1 %all-to-all-start.2 = ((bf16[16,16,1024]{2,1,0:T(8,128)(2,1)}), bf16[16,16,1024]{2,1,0:T(8,128)(2,1)S(1)}, u32[]{:S(2)}, u32[]{:S(2)}) async-start(bf16[16,16,1024]{2,1,0:T(8,128)(2,1)} %bitcast.3), calls=%async_computation.2 | async-start | bytes 1048576 | tf_op jit(solution)/shard_map/all_to_all | solution.py:140
  655.8 58.1 %copy-start.27 = (bf16[16,1024]{1,0:T(8,128)(2,1)S(1)}, bf16[16,1024]{1,0:T(8,128)(2,1)}, u32[]{:S(2)}) copy-start(bf16[16,1024]{1,0:T(8,128)(2,1)} %param.36) | copy-start | bytes 98308
  667.5 46.2 %all-to-all-start.3 = ((bf16[32,16,1024]{2,1,0:T(8,128)(2,1)}), bf16[32,16,1024]{2,1,0:T(8,128)(2,1)S(1)}, u32[]{:S(2)}, u32[]{:S(2)}) async-start(bf16[32,16,1024]{2,1,0:T(8,128)(2,1)} %bitcast.4), calls=%async_computation.3 | async-start | bytes 2097152 | tf_op jit(solution)/shard_map/all_to_all | solution.py:144
  (20 other events, 19.4 us)
Sparse Core Ops, SparseCore 0:
  243.8 152.1 all-gather.2
  483.6 142.3 all-gather.4
where the time goes:
time: 723 us; the launch traced here: 721 us
  waiting for transfers between devices  312 us (43%)
  blocking collectives  278 us (38%)
  starting transfers between devices  49.1 us (7%)
  local copies, waits for them, and re-layouts  26 us (4%)
  between operations  20.4 us (3%)
  other arithmetic  18.2 us (3%)
  matrix products  17.9 us (2%)
    all_gather x2, waiting for transfers between devices, shards(): lax.all_gather(scaled, 'row', axis=0, tiled=True)  231 us
    unnamed x2, blocking collectives  116 us
    all_gather x1, blocking collectives, shards(): col_gathered = lax.all_gather(unit_vecs, 'row', axis=0, tiled=True)  67.6 us
    all_gather x2, blocking collectives, shards(): row_labels = lax.all_gather(scaled, 'col', axis=0, tiled=True)  59.1 us
    all_to_all x2, waiting for transfers between devices, shards(): lax.all_to_all(sent_cols, 'row', split_axis=0, concat_axis=0, tiled=True)  57.5 us
    all_gather x1, blocking collectives, shards(): row_units = lax.all_gather(unit_vecs, 'col', axis=0, tiled=True)  35.3 us
    all_to_all x2, starting transfers between devices, shards(): lax.all_to_all(sent_cols, 'row', split_axis=0, concat_axis=0, tiled=True)  34.8 us
    all_to_all x2, waiting for transfers between devices, shards(): lax.all_to_all(sent_rows, 'col', split_axis=0, concat_axis=0, tiled=True)  23.4 us
  transfers between devices with their start and end apart: 6, of which 6 were waited for; matrix products, arithmetic and copies ran while one was open for 1% of the time, Pallas kernels for 0%

commit v1 on v0

--- a/solution.py
+++ b/solution.py
@@ -121,7 +121,22 @@
     current = seed_scores
     for iteration in range(ITERS):
         scaled = (inv_root[:, None] * current).astype(jnp.bfloat16)
-        col_labels = rotate_rows(lax.all_gather(scaled, "row", axis=0, tiled=True), shift)
+
+        def settle_the_tables(in_array, device_axis="row"):
+            h_now = jnp.concatenate(
+                jax.lax.all_to_all(
+                    jnp.stack(
+                        tuple((in_array for _ in range(jax.lax.axis_size(device_axis)))), axis=0
+                    ),
+                    device_axis,
+                    0,
+                    0,
+                ),
+                0,
+            )
+            return h_now
+
+        col_labels = rotate_rows(settle_the_tables(scaled), shift)
         row_sum = jnp.zeros((row_total, channels), jnp.float32)
         col_parts = []
         row_labels = lax.all_gather(scaled, "col", axis=0, tiled=True)

time: 723 us -> 506 us (0.70)
  waiting for transfers between devices: 312 us -> 79.2 us
  blocking collectives: 278 us -> 303 us
  between operations: 20.4 us -> 7.16 us
    all_gather x2 -> x0, waiting for transfers between devices: 231 us -> none  [shards(): lax.all_gather(scaled, 'row', axis=0, tiled=True)]
    all_gather x2, blocking collectives: 59.1 us -> 84.5 us  [shards(): row_labels = lax.all_gather(scaled, 'col', axis=0, tiled=True)]
    all_to_all x0 -> x2, starting transfers between devices: none -> 24.6 us  [settle_the_tables(): jax.lax.all_to_all(jnp.stack(tuple((in_array for _ in range(jax.lax.axis_...]
    all_to_all x2, starting transfers between devices: 34.8 us -> 19 us  [shards(): lax.all_to_all(sent_cols, 'row', split_axis=0, concat_axis=0, tiled=True)]
    unnamed x109 -> x115, local copies, waits for them, and re-layouts: 18 us -> 20 us
  transfers between devices with their start and end apart: 6 -> 6, of which waited for: 6 -> 4; matrix products, arithmetic and copies ran while one was open for 1% -> 1% of each run, Pallas kernels for 0% -> 0%
where the time goes in v1:
time: 506 us; the launch traced here: 504 us
  blocking collectives  303 us (60%)
  waiting for transfers between devices  79.2 us (16%)
  starting transfers between devices  50.8 us (10%)
  local copies, waits for them, and re-layouts  28.4 us (6%)
  matrix products  19.3 us (4%)
  other arithmetic  15.6 us (3%)
  between operations  7.16 us (1%)
    unnamed x2, blocking collectives  116 us
    all_gather x2, blocking collectives, shards(): row_labels = lax.all_gather(scaled, 'col', axis=0, tiled=True)  84.5 us
    all_gather x1, blocking collectives, shards(): col_gathered = lax.all_gather(unit_vecs, 'row', axis=0, tiled=True)  67.6 us
    all_to_all x2, waiting for transfers between devices, shards(): lax.all_to_all(sent_cols, 'row', split_axis=0, concat_axis=0, tiled=True)  56.1 us
    all_gather x1, blocking collectives, shards(): row_units = lax.all_gather(unit_vecs, 'col', axis=0, tiled=True)  35.3 us
    all_to_all x2, starting transfers between devices, settle_the_tables(): jax.lax.all_to_all(jnp.stack(tuple((in_array for _ in range(jax.lax.axis_...  24.6 us
    all_to_all x2, waiting for transfers between devices, shards(): lax.all_to_all(sent_rows, 'col', split_axis=0, concat_axis=0, tiled=True)  23.1 us
    unnamed x115, local copies, waits for them, and re-layouts  20 us
  transfers between devices with their start and end apart: 6, of which 4 were waited for; matrix products, arithmetic and copies ran while one was open for 1% of the time, Pallas kernels for 0%

profile of v1, /device:TPU:16, one launch (start us, length us, event | category | flops | bytes accessed | tf_op | source)
XLA Modules:
  0.0 504.1 jit_solution(16850610361621237555)
XLA Ops:
  1.6 35.3 %all_gather.12 = bf16[256,256]{1,0:T(8,128)(2,1)S(1)} all-gather(bf16[16,256]{1,0:T(8,128)(2,1)S(1)} %fusion.91), channel_id=1, replica_groups=mesh['row'=32,'col'=16] {'col'}, dimensions={0}, use_global_device_ids=true | all-gather | bytes 139264 | tf_op jit(solution)/shard_map/all_gather | solution.py:63
  36.9 67.6 %all_gather.13 = bf16[512,256]{1,0:T(8,128)(2,1)S(1)} all-gather(bf16[16,256]{1,0:T(8,128)(2,1)S(1)} %fusion.91), channel_id=1, replica_groups=mesh['row'=32,'col'=16] {'row'}, dimensions={0}, use_global_device_ids=true | all-gather | bytes 270336 | tf_op jit(solution)/shard_map/all_gather | solution.py:64
  105.8 1.3 dynamic-slice
  120.5 73.2 %all-reduce.1 = f32[512]{0:T(512)S(1)} all-reduce(f32[512]{0:T(512)S(1)} %dynamic_slice.19), channel_id=3, replica_groups=mesh['row'=32,'col'=16] {'row'}, use_global_device_ids=true, to_apply=%region_18.19.clone | all-reduce | flops 512 | bytes 4096
  193.6 42.8 %all-reduce = f32[256]{0:T(256)S(1)} all-reduce(f32[256]{0:T(256)S(1)} %add_add_fusion), channel_id=2, replica_groups=mesh['row'=32,'col'=16] {'col'}, use_global_device_ids=true, to_apply=%region_9.10.clone | all-reduce | flops 256 | bytes 2048
  237.7 19.9 %all-to-all-start = ((bf16[32,16,1024]{2,1,0:T(8,128)(2,1)}), bf16[32,16,1024]{2,1,0:T(8,128)(2,1)S(1)}, u32[]{:S(2)}, u32[]{:S(2)}) async-start(bf16[32,16,1024]{2,1,0:T(8,128)(2,1)} %stack.4), calls=%async_computation | async-start | bytes 2097152 | tf_op jit(solution)/shard_map/all_to_all | solution.py:127
  262.5 39.2 %all_gather.14 = bf16[256,1024]{1,0:T(8,128)(2,1)S(1)} all-gather(bf16[16,1024]{1,0:T(8,128)(2,1)S(1)} %fusion.72), channel_id=1, replica_groups=mesh['row'=32,'col'=16] {'col'}, dimensions={0}, use_global_device_ids=true | all-gather | bytes 557056 | tf_op jit(solution)/shard_map/all_gather | solution.py:142
  310.9 2.0 conditional.21
  313.9 1.8 conditional.22
  315.7 4.7 add_convert_fusion.1
  320.4 3.6 all-to-all-start.1
  327.1 11.6 %all-to-all-done.1 = bf16[16,16,1024]{2,1,0:T(8,128)(2,1)S(1)} async-done(((bf16[16,16,1024]{2,1,0:T(8,128)(2,1)}), bf16[16,16,1024]{2,1,0:T(8,128)(2,1)S(1)}, u32[]{:S(2)}, u32[]{:S(2)}) %all-to-all-start.1) | async-done | bytes 524320 | tf_op jit(solution)/shard_map/all_to_all | solution.py:155
  338.7 10.2 %all-to-all-start.2 = ((bf16[32,16,1024]{2,1,0:T(8,128)(2,1)}), bf16[32,16,1024]{2,1,0:T(8,128)(2,1)S(1)}, u32[]{:S(2)}, u32[]{:S(2)}) async-start(bf16[32,16,1024]{2,1,0:T(8,128)(2,1)} %bitcast.3), calls=%async_computation.2 | async-start | bytes 2097152 | tf_op jit(solution)/shard_map/all_to_all | solution.py:159
  349.0 28.1 %all-to-all-done.2 = bf16[32,16,1024]{2,1,0:T(8,128)(2,1)S(1)} async-done(((bf16[32,16,1024]{2,1,0:T(8,128)(2,1)}), bf16[32,16,1024]{2,1,0:T(8,128)(2,1)S(1)}, u32[]{:S(2)}, u32[]{:S(2)}) %all-to-all-start.2) | async-done | bytes 1048608 | tf_op jit(solution)/shard_map/all_to_all | solution.py:159
  378.4 4.7 all-to-all-start.3
  383.2 45.4 %all_gather.15 = bf16[256,1024]{1,0:T(8,128)(2,1)S(1)} all-gather(bf16[16,1024]{1,0:T(8,128)(2,1)S(1)} %fusion.70), channel_id=1, replica_groups=mesh['row'=32,'col'=16] {'col'}, dimensions={0}, use_global_device_ids=true | all-gather | bytes 557056 | tf_op jit(solution)/shard_map/all_gather | solution.py:142
  428.6 1.3 fusion.64
  438.5 2.0 conditional.29
  441.5 1.8 conditional.30
  443.3 4.7 add_convert_fusion
  448.0 3.6 all-to-all-start.4
  454.8 11.6 %all-to-all-done.4 = bf16[16,16,1024]{2,1,0:T(8,128)(2,1)S(1)} async-done(((bf16[16,16,1024]{2,1,0:T(8,128)(2,1)}), bf16[16,16,1024]{2,1,0:T(8,128)(2,1)S(1)}, u32[]{:S(2)}, u32[]{:S(2)}) %all-to-all-start.4) | async-done | bytes 524320 | tf_op jit(solution)/shard_map/all_to_all | solution.py:155
  466.3 8.7 %all-to-all-start.5 = ((bf16[32,16,1024]{2,1,0:T(8,128)(2,1)}), bf16[32,16,1024]{2,1,0:T(8,128)(2,1)S(1)}, u32[]{:S(2)}, u32[]{:S(2)}) async-start(bf16[32,16,1024]{2,1,0:T(8,128)(2,1)} %bitcast.6), calls=%async_computation.5 | async-start | bytes 2097152 | tf_op jit(solution)/shard_map/all_to_all | solution.py:159
  475.1 28.1 %all-to-all-done.5 = bf16[32,16,1024]{2,1,0:T(8,128)(2,1)S(1)} async-done(((bf16[32,16,1024]{2,1,0:T(8,128)(2,1)}), bf16[32,16,1024]{2,1,0:T(8,128)(2,1)S(1)}, u32[]{:S(2)}, u32[]{:S(2)}) %all-to-all-start.5) | async-done | bytes 1048608 | tf_op jit(solution)/shard_map/all_to_all | solution.py:159
  (203 shorter events, 57.0 us)
Async XLA Ops:
  112.1 124.4 %copy-start.24 = (bf16[16,1024]{1,0:T(8,128)(2,1)S(1)}, bf16[16,1024]{1,0:T(8,128)(2,1)}, u32[]{:S(2)}) copy-start(bf16[16,1024]{1,0:T(8,128)(2,1)} %param.36) | copy-start | bytes 98308
  117.8 119.8 %copy-start.12 = (bf16[256,64]{0,1:T(8,128)(2,1)}, bf16[256,64]{0,1:T(8,128)(2,1)S(1)}, u32[]{:S(2)}) copy-start(bf16[256,64]{0,1:T(8,128)(2,1)S(1)} %fusion.57) | copy-start | bytes 98308
  118.1 119.6 %copy-start.13 = (bf16[256,64]{0,1:T(8,128)(2,1)}, bf16[256,64]{0,1:T(8,128)(2,1)S(1)}, u32[]{:S(2)}) copy-start(bf16[256,64]{0,1:T(8,128)(2,1)S(1)} %fusion.58) | copy-start | bytes 98308
  118.3 190.0 %copy-start.14 = (bf16[256,64]{0,1:T(8,128)(2,1)}, bf16[256,64]{0,1:T(8,128)(2,1)S(1)}, u32[]{:S(2)}) copy-start(bf16[256,64]{0,1:T(8,128)(2,1)S(1)} %fusion.59) | copy-start | bytes 98308
  118.5 188.3 %copy-start.16 = (bf16[256,64]{0,1:T(8,128)(2,1)}, bf16[256,64]{0,1:T(8,128)(2,1)S(1)}, u32[]{:S(2)}) copy-start(bf16[256,64]{0,1:T(8,128)(2,1)S(1)} %fusion.60) | copy-start | bytes 98308
  118.7 186.5 %copy-start.18 = (bf16[256,64]{0,1:T(8,128)(2,1)}, bf16[256,64]{0,1:T(8,128)(2,1)S(1)}, u32[]{:S(2)}) copy-start(bf16[256,64]{0,1:T(8,128)(2,1)S(1)} %fusion.61) | copy-start | bytes 98308
  118.9 184.8 %copy-start.20 = (bf16[256,64]{0,1:T(8,128)(2,1)}, bf16[256,64]{0,1:T(8,128)(2,1)S(1)}, u32[]{:S(2)}) copy-start(bf16[256,64]{0,1:T(8,128)(2,1)S(1)} %fusion.62) | copy-start | bytes 98308
  119.1 184.0 %copy-start.22 = (bf16[256,64]{0,1:T(8,128)(2,1)}, bf16[256,64]{0,1:T(8,128)(2,1)S(1)}, u32[]{:S(2)}) copy-start(bf16[256,64]{0,1:T(8,128)(2,1)S(1)} %fusion.63) | copy-start | bytes 98308
  120.2 182.8 %copy-start.27 = (bf16[256,64]{0,1:T(8,128)(2,1)}, bf16[256,64]{0,1:T(8,128)(2,1)S(1)}, u32[]{:S(2)}) copy-start(bf16[256,64]{0,1:T(8,128)(2,1)S(1)} %get-tuple-element.486) | copy-start | bytes 98308
  120.2 182.8 %copy-start.39 = (bf16[256,64]{0,1:T(8,128)(2,1)}, bf16[256,64]{0,1:T(8,128)(2,1)S(1)}, u32[]{:S(2)}) copy-start(bf16[256,64]{0,1:T(8,128)(2,1)S(1)} %get-tuple-element.424) | copy-start | bytes 98308
  120.3 182.9 %copy-start.37 = (bf16[256,64]{0,1:T(8,128)(2,1)}, bf16[256,64]{0,1:T(8,128)(2,1)S(1)}, u32[]{:S(2)}) copy-start(bf16[256,64]{0,1:T(8,128)(2,1)S(1)} %get-tuple-element.483) | copy-start | bytes 98308
  120.3 183.5 %copy-start.35 = (bf16[256,64]{0,1:T(8,128)(2,1)}, bf16[256,64]{0,1:T(8,128)(2,1)S(1)}, u32[]{:S(2)}) copy-start(bf16[256,64]{0,1:T(8,128)(2,1)S(1)} %get-tuple-element.465) | copy-start | bytes 98308
  120.3 185.0 %copy-start.33 = (bf16[256,64]{0,1:T(8,128)(2,1)}, bf16[256,64]{0,1:T(8,128)(2,1)S(1)}, u32[]{:S(2)}) copy-start(bf16[256,64]{0,1:T(8,128)(2,1)S(1)} %get-tuple-element.468) | copy-start | bytes 98308
  120.3 186.5 %copy-start.31 = (bf16[256,64]{0,1:T(8,128)(2,1)}, bf16[256,64]{0,1:T(8,128)(2,1)S(1)}, u32[]{:S(2)}) copy-start(bf16[256,64]{0,1:T(8,128)(2,1)S(1)} %get-tuple-element.471) | copy-start | bytes 98308
  120.3 188.0 %copy-start.29 = (bf16[256,64]{0,1:T(8,128)(2,1)}, bf16[256,64]{0,1:T(8,128)(2,1)S(1)}, u32[]{:S(2)}) copy-start(bf16[256,64]{0,1:T(8,128)(2,1)S(1)} %get-tuple-element.474) | copy-start | bytes 98308
  237.7 64.0 %all-to-all-start = ((bf16[32,16,1024]{2,1,0:T(8,128)(2,1)}), bf16[32,16,1024]{2,1,0:T(8,128)(2,1)S(1)}, u32[]{:S(2)}, u32[]{:S(2)}) async-start(bf16[32,16,1024]{2,1,0:T(8,128)(2,1)} %stack.4), calls=%async_computation | async-start | bytes 2097152 | tf_op jit(solution)/shard_map/all_to_all | solution.py:127
  320.4 18.3 %all-to-all-start.1 = ((bf16[16,16,1024]{2,1,0:T(8,128)(2,1)}), bf16[16,16,1024]{2,1,0:T(8,128)(2,1)S(1)}, u32[]{:S(2)}, u32[]{:S(2)}) async-start(bf16[16,16,1024]{2,1,0:T(8,128)(2,1)} %bitcast.2), calls=%async_computation.1 | async-start | bytes 1048576 | tf_op jit(solution)/shard_map/all_to_all | solution.py:155
  327.1 50.1 %copy-start.25 = (bf16[16,1024]{1,0:T(8,128)(2,1)S(1)}, bf16[16,1024]{1,0:T(8,128)(2,1)}, u32[]{:S(2)}) copy-start(bf16[16,1024]{1,0:T(8,128)(2,1)} %param.36) | copy-start | bytes 98308
  338.7 38.4 %all-to-all-start.2 = ((bf16[32,16,1024]{2,1,0:T(8,128)(2,1)}), bf16[32,16,1024]{2,1,0:T(8,128)(2,1)S(1)}, u32[]{:S(2)}, u32[]{:S(2)}) async-start(bf16[32,16,1024]{2,1,0:T(8,128)(2,1)} %bitcast.3), calls=%async_computation.2 | async-start | bytes 2097152 | tf_op jit(solution)/shard_map/all_to_all | solution.py:159
  378.4 51.4 %copy-start.28 = (bf16[256,64]{0,1:T(8,128)(2,1)S(1)}, bf16[256,64]{0,1:T(8,128)(2,1)}, u32[]{:S(2)}) copy-start(bf16[256,64]{0,1:T(8,128)(2,1)} %copy-done.27) | copy-start | bytes 98308
  378.4 51.4 %copy-start.40 = (bf16[256,64]{0,1:T(8,128)(2,1)S(1)}, bf16[256,64]{0,1:T(8,128)(2,1)}, u32[]{:S(2)}) copy-start(bf16[256,64]{0,1:T(8,128)(2,1)} %copy-done.39) | copy-start | bytes 98308
  378.4 50.1 %all-to-all-start.3 = ((bf16[32,16,1024]{2,1,0:T(8,128)(2,1)}), bf16[32,16,1024]{2,1,0:T(8,128)(2,1)S(1)}, u32[]{:S(2)}, u32[]{:S(2)}) async-start(bf16[32,16,1024]{2,1,0:T(8,128)(2,1)} %stack.5), calls=%async_computation.3 | async-start | bytes 2097152 | tf_op jit(solution)/shard_map/all_to_all | solution.py:127
  448.0 18.3 %all-to-all-start.4 = ((bf16[16,16,1024]{2,1,0:T(8,128)(2,1)}), bf16[16,16,1024]{2,1,0:T(8,128)(2,1)S(1)}, u32[]{:S(2)}, u32[]{:S(2)}) async-start(bf16[16,16,1024]{2,1,0:T(8,128)(2,1)} %bitcast.5), calls=%async_computation.4 | async-start | bytes 1048576 | tf_op jit(solution)/shard_map/all_to_all | solution.py:155
  466.3 36.9 %all-to-all-start.5 = ((bf16[32,16,1024]{2,1,0:T(8,128)(2,1)}), bf16[32,16,1024]{2,1,0:T(8,128)(2,1)S(1)}, u32[]{:S(2)}, u32[]{:S(2)}) async-start(bf16[32,16,1024]{2,1,0:T(8,128)(2,1)} %bitcast.6), calls=%async_computation.5 | async-start | bytes 2097152 | tf_op jit(solution)/shard_map/all_to_all | solution.py:159
  (23 other events, 70.7 us)
